TPU v7x, 32 devices: a whole 2x2x4 slice. The times are simulated.
32 devices in a mesh: pair: 8 (over z, x), col: 4 (over y, core).
Axes of the slice: x: 2, y: 2, z: 4, core: 2. Of those that a mesh axis runs over, the one named last changes fastest.
Arguments:
- point_values: bfloat16 [32768, 1024], P('pair', 'col'), may hold values from -2 to 2, as said below
- grid_values: bfloat16 [32768, 512], P('pair'), may hold values from -6 to 6
Outputs:
- fitted: float32 [512, 1024], P(('pair', 'col'))
Inputs may be any that keep to these rules, and one draw needn't show every extreme that they name: `point_values`: real pair-product values.
All inputs are finite; a program needn't handle non-finite values.
Results may differ from a plain program's by a relative error of at most 0.0003.
Values may be sent and summed in bfloat16 or wider, within the bound.
A program may use at most 128 MiB of HBM per device.

v0:
```python
import jax
import jax.numpy as jnp
from jax import lax
from jax.sharding import PartitionSpec as P


def cross(left, right):
    return lax.dot_general(
        left, right, (((0,), (0,)), ((), ())), preferred_element_type=jnp.float32
    )


def body(point_values, grid_values):
    gathered = lax.all_gather(point_values, "col", axis=1, tiled=True)
    gram = lax.psum(cross(gathered, gathered), "pair")
    factor = jnp.linalg.cholesky(gram)
    summed = lax.psum_scatter(
        cross(grid_values, point_values), "pair", scatter_dimension=0, tiled=True
    )
    regrouped = lax.all_to_all(summed, "col", split_axis=0, concat_axis=1, tiled=True)
    solved = jax.scipy.linalg.cho_solve((factor, True), regrouped.T)
    return solved.T


def solution(mesh):
    in_specs = (P("pair", "col"), P("pair", None))
    out_specs = P(("pair", "col"), None)
    return jax.shard_map(body, mesh=mesh, in_specs=in_specs, out_specs=out_specs, check_vma=False)
```

profile of v0, /device:TPU:0, one launch (start us, length us, event | category | flops | bytes accessed | tf_op | source)
XLA Modules:
  0.0 594.1 jit_solution(14145770324071007327)
XLA Ops:
  8.1 5.0 fusion.96
  13.2 58.8 %all-gather.2.cloned.1.call-done = bf16[4096,1024]{1,0:T(8,128)(2,1)} async-done(((bf16[4096,256]{1,0:T(8,128)(2,1)}), bf16[4096,1024]{1,0:T(8,128)(2,1)}) %all-gather.2.cloned.1.call-update) | async-done | bytes 8388624 | tf_op jit(solution)/shard_map/all_gather | solution.py:14
  72.0 15.1 %fusion.95 = f32[1024,1024]{0,1:T(8,128)} fusion(bf16[4096,1024]{1,0:T(8,128)(2,1)} %all-gather.2.cloned.1.call-done), kind=kOutput, calls=%fused_computation.213 | convolution fusion | flops 8589934592 | bytes 12582912 | tf_op jit(solution)/shard_map/dot_general | solution.py:8
  87.1 3.3 all-to-all-start
  90.4 4.1 all-to-all-done
  94.5 148.8 %all-reduce.3.cloned.1.call-done = f32[1024,1024]{0,1:T(8,128)} async-done(((f32[1024,1024]{0,1:T(8,128)}), f32[1024,1024]{0,1:T(8,128)}) %all-reduce.3.cloned.1.call-update) | async-done | bytes 4194320 | tf_op jit(solution)/shard_map/psum | solution.py:15
  243.3 5.6 copy.9
  248.9 4.4 fusion
  255.3 11.7 %cholesky.223 = f32[128,128]{1,0:T(8,128)S(1)} custom-call(f32[128,128]{1,0:T(8,128)S(1)} %cholesky.580), custom_call_target="Cholesky" | custom-call | tf_op jit(solution)/shard_map/jit(cholesky)/cholesky | solution.py:16
  267.0 9.8 %custom-call.66 = f32[1,128,128]{1,2,0:T(8,128)S(1)} custom-call(f32[1,128,128]{2,1,0:T(8,128)S(1)} %get-tuple-element.44), custom_call_target="InvertDiagBlocksLowerTriangular" | custom-call | tf_op jit(solution)/shard_map/jit(cholesky)/cholesky | solution.py:16
  276.9 2.5 cholesky.255
  279.4 2.4 constant_dynamic-update-slice_fusion.50
  283.3 12.2 %cholesky.244 = f32[128,128]{1,0:T(8,128)S(1)} custom-call(f32[128,128]{1,0:T(8,128)S(1)} %cholesky.584), custom_call_target="Cholesky" | custom-call | tf_op jit(solution)/shard_map/jit(cholesky)/cholesky | solution.py:16
  296.2 9.8 %custom-call.67 = f32[1,128,128]{1,2,0:T(8,128)S(1)} custom-call(f32[1,128,128]{2,1,0:T(8,128)S(1)} %get-tuple-element.41), custom_call_target="InvertDiagBlocksLowerTriangular" | custom-call | tf_op jit(solution)/shard_map/jit(cholesky)/cholesky | solution.py:16
  309.3 11.7 %cholesky.468 = f32[128,128]{1,0:T(8,128)S(1)} custom-call(f32[128,128]{1,0:T(8,128)S(1)} %cholesky.589), custom_call_target="Cholesky" | custom-call | tf_op jit(solution)/shard_map/jit(cholesky)/cholesky | solution.py:16
  322.3 9.8 %custom-call.68 = f32[1,128,128]{1,2,0:T(8,128)S(1)} custom-call(f32[1,128,128]{2,1,0:T(8,128)S(1)} %get-tuple-element.38), custom_call_target="InvertDiagBlocksLowerTriangular" | custom-call | tf_op jit(solution)/shard_map/jit(cholesky)/cholesky | solution.py:16
  333.3 2.3 convolution_subtract_fusion.2
  335.6 11.8 %cholesky.487 = f32[128,128]{1,0:T(8,128)S(1)} custom-call(f32[128,128]{1,0:T(8,128)S(1)} %cholesky.594), custom_call_target="Cholesky" | custom-call | tf_op jit(solution)/shard_map/jit(cholesky)/cholesky | solution.py:16
  348.8 9.8 %custom-call.69 = f32[1,128,128]{1,2,0:T(8,128)S(1)} custom-call(f32[1,128,128]{2,1,0:T(8,128)S(1)} %get-tuple-element.35), custom_call_target="InvertDiagBlocksLowerTriangular" | custom-call | tf_op jit(solution)/shard_map/jit(cholesky)/cholesky | solution.py:16
  359.7 2.3 convolution_subtract_fusion.3
  362.0 11.7 %cholesky.506 = f32[128,128]{1,0:T(8,128)S(1)} custom-call(f32[128,128]{1,0:T(8,128)S(1)} %cholesky.599), custom_call_target="Cholesky" | custom-call | tf_op jit(solution)/shard_map/jit(cholesky)/cholesky | solution.py:16
  375.0 10.0 %custom-call.70 = f32[1,128,128]{1,2,0:T(8,128)S(1)} custom-call(f32[1,128,128]{2,1,0:T(8,128)S(1)} %get-tuple-element.32), custom_call_target="InvertDiagBlocksLowerTriangular" | custom-call | tf_op jit(solution)/shard_map/jit(cholesky)/cholesky | solution.py:16
  386.0 2.3 convolution_subtract_fusion.4
  388.3 11.7 %cholesky.526 = f32[128,128]{1,0:T(8,128)S(1)} custom-call(f32[128,128]{1,0:T(8,128)S(1)} %cholesky.604), custom_call_target="Cholesky" | custom-call | tf_op jit(solution)/shard_map/jit(cholesky)/cholesky | solution.py:16
  401.3 9.8 %custom-call.71 = f32[1,128,128]{1,2,0:T(8,128)S(1)} custom-call(f32[1,128,128]{2,1,0:T(8,128)S(1)} %get-tuple-element.29), custom_call_target="InvertDiagBlocksLowerTriangular" | custom-call | tf_op jit(solution)/shard_map/jit(cholesky)/cholesky | solution.py:16
  414.1 12.1 %cholesky.546 = f32[128,128]{1,0:T(8,128)S(1)} custom-call(f32[128,128]{1,0:T(8,128)S(1)} %cholesky.609), custom_call_target="Cholesky" | custom-call | tf_op jit(solution)/shard_map/jit(cholesky)/cholesky | solution.py:16
  427.5 9.8 %custom-call.72 = f32[1,128,128]{1,2,0:T(8,128)S(1)} custom-call(f32[1,128,128]{2,1,0:T(8,128)S(1)} %get-tuple-element.26), custom_call_target="InvertDiagBlocksLowerTriangular" | custom-call | tf_op jit(solution)/shard_map/jit(cholesky)/cholesky | solution.py:16
  439.9 11.7 %cholesky.564 = f32[128,128]{1,0:T(8,128)S(1)} custom-call(f32[128,128]{1,0:T(8,128)S(1)} %convolution_subtract_fusion.6), custom_call_target="Cholesky" | custom-call | tf_op jit(solution)/shard_map/jit(cholesky)/cholesky | solution.py:16
  458.5 4.8 select_select_fusion
  463.2 22.8 %while.1 = (s32[]{:T(128)}, f32[1024,1024]{1,0:T(8,128)}, s32[8,2]{0,1:T(2,128)S(1)}, f32[8,128,128]{2,1,0:T(8,128)S(1)}, s32[]{:T(128)}) while((s32[]{:T(128)}, f32[1024,1024]{1,0:T(8,128)}, s32[8,2]{0,1:T(2,128)S(1)}, f32[8,128,128]{2,1,0:T(8,128)S(1)}, s32[]{:T(128)}) %tuple.56), condition=%wide.while_cond, body=%wide.while_body.sunk | while | flops 2 | bytes 131181 | solution.py:21
  469.6 2.2 bitcast_dynamic-update-slice_fusion.2
  486.1 78.8 %custom-call.73 = f32[8,128,128]{1,2,0:T(8,128)S(1)} custom-call(f32[8,128,128]{2,1,0:T(8,128)S(1)} %get-tuple-element.12), custom_call_target="InvertDiagBlocksLowerTriangular" | custom-call | tf_op jit(solution)/shard_map/jit(_cho_solve)/triangular_solve | solution.py:21
  (122 shorter events, 67.5 us)
Async XLA Ops:
  7.4 64.6 %all-gather.2.cloned.1.call-start = ((), (), s32[]{:S(2)}) async-start(), calls=%async_computation.2 | async-start | bytes 10485760 | tf_op jit(solution)/shard_map/all_gather | solution.py:14
  8.1 79.0 %reduce-scatter.2.cloned.1.call-start = ((), (), s32[]{:S(2)}) async-start(), calls=%async_computation.4 | async-start | bytes 589824 | tf_op jit(solution)/shard_map/reduce_scatter | solution.py:17
  13.1 230.2 %all-reduce.3.cloned.1.call-start = ((), (), s32[]{:S(2)}) async-start(), calls=%async_computation.3 | async-start | bytes 8388608 | tf_op jit(solution)/shard_map/psum | solution.py:15
  87.1 7.4 %all-to-all-start = ((f32[4,16,256]{2,1,0:T(8,128)}), f32[4,16,256]{2,1,0:T(8,128)S(1)}, u32[]{:S(2)}, u32[]{:S(2)}) async-start(f32[4,16,256]{2,1,0:T(8,128)} %bitcast.147), calls=%async_computation.1 | async-start | bytes 131072 | tf_op jit(solution)/shard_map/all_to_all | solution.py:20
  253.4 1.9 copy-start
  585.8 0.6 copy-start.1
Sparse Core Ops, SparseCore 0:
  9.8 62.1 all-gather.1
Sparse Core Ops, SparseCore 1:
  13.2 64.7 reduce-scatter.1
  87.2 156.1 all-reduce.2
where the time goes:
time: 600 us; the launch traced here: 594 us
  other arithmetic  261 us (44%)
  waiting for transfers between devices  212 us (35%)
  matrix products  63.6 us (11%)
  local copies, waits for them, and re-layouts  33.6 us (6%)
  between operations  20.3 us (3%)
    another operation x30, other arithmetic, body(): factor = jnp.linalg.cholesky(gram)  173 us
    psum x1, waiting for transfers between devices, body(): gram = lax.psum(cross(gathered, gathered), 'pair')  149 us
    another operation x3, other arithmetic, body(): solved = jax.scipy.linalg.cho_solve((factor, True), regrouped.T)  83.6 us
    all_gather x1, waiting for transfers between devices, body(): gathered = lax.all_gather(point_values, 'col', axis=1, tiled=True)  58.8 us
    another operation x14, matrix products, body(): factor = jnp.linalg.cholesky(gram)  23.1 us
    another operation x24, local copies, waits for them, and re-layouts  22.7 us
    another operation x30, matrix products, body(): solved = jax.scipy.linalg.cho_solve((factor, True), regrouped.T)  20.5 us
    dot_general x2, matrix products, cross(): lax.dot_general(left, right, (((0,), (0,)), ((), ())), preferred_element_...  20 us
  transfers between devices with their start and end apart: 4, of which 3 were waited for; matrix products, arithmetic and copies ran while one was open for 3% of the time, Pallas kernels for 0%

commit v1 on v0

--- a/solution.py
+++ b/solution.py
@@ -12,7 +12,7 @@
 
 def body(point_values, grid_values):
     gathered = lax.all_gather(point_values, "col", axis=1, tiled=True)
-    gram = lax.psum(cross(gathered, gathered), "pair")
+    gram = jnp.sum(lax.all_gather(cross(gathered, gathered), "pair"), axis=0)
     factor = jnp.linalg.cholesky(gram)
     summed = lax.psum_scatter(
         cross(grid_values, point_values), "pair", scatter_dimension=0, tiled=True

time: 600 us -> 1100 us (1.83)
  waiting for transfers between devices: 212 us -> 694 us
  other arithmetic: 261 us -> 275 us
    all_gather x0 -> x1, waiting for transfers between devices: none -> 630 us  [body(): gram = jnp.sum(lax.all_gather(cross(gathered, gathered), 'pair'), axis=0)]
    psum x1 -> x0, waiting for transfers between devices: 149 us -> none  [body(): gram = lax.psum(cross(gathered, gathered), 'pair')]
    reduce_sum x0 -> x1, other arithmetic: none -> 14.7 us  [body(): gram = jnp.sum(lax.all_gather(cross(gathered, gathered), 'pair'), axis=0)]
  transfers between devices with their start and end apart: 4 -> 4, of which waited for: 3 -> 3; matrix products, arithmetic and copies ran while one was open for 3% -> 2% of each run, Pallas kernels for 0% -> 0%
where the time goes in v1:
time: 1100 us; the launch traced here: 1090 us
  waiting for transfers between devices  694 us (63%)
  other arithmetic  275 us (25%)
  matrix products  63.7 us (6%)
  local copies, waits for them, and re-layouts  33.6 us (3%)
  between operations  20.3 us (2%)
    all_gather x1, waiting for transfers between devices, body(): gram = jnp.sum(lax.all_gather(cross(gathered, gathered), 'pair'), axis=0)  630 us
    another operation x30, other arithmetic, body(): factor = jnp.linalg.cholesky(gram)  173 us
    another operation x3, other arithmetic, body(): solved = jax.scipy.linalg.cho_solve((factor, True), regrouped.T)  83.6 us
    all_gather x1, waiting for transfers between devices, body(): gathered = lax.all_gather(point_values, 'col', axis=1, tiled=True)  58.8 us
    another operation x14, matrix products, body(): factor = jnp.linalg.cholesky(gram)  23.1 us
    another operation x24, local copies, waits for them, and re-layouts  22.7 us
  transfers between devices with their start and end apart: 4, of which 3 were waited for; matrix products, arithmetic and copies ran while one was open for 2% of the time, Pallas kernels for 0%

profile of v1, /device:TPU:0, one launch (start us, length us, event | category | flops | bytes accessed | tf_op | source)
XLA Modules:
  0.0 1090.5 jit_solution(5713015690415199770)
XLA Ops:
  8.1 5.0 fusion.96
  13.2 58.8 %all-gather.4.cloned.1.call-done = bf16[4096,1024]{1,0:T(8,128)(2,1)} async-done(((bf16[4096,256]{1,0:T(8,128)(2,1)}), bf16[4096,1024]{1,0:T(8,128)(2,1)}) %all-gather.4.cloned.1.call-update) | async-done | bytes 8388624 | tf_op jit(solution)/shard_map/all_gather | solution.py:14
  72.0 15.2 %fusion.95 = f32[1024,1024]{1,0:T(8,128)} fusion(bf16[4096,1024]{1,0:T(8,128)(2,1)} %all-gather.4.cloned.1.call-done), kind=kOutput, calls=%fused_computation.213 | convolution fusion | flops 8589934592 | bytes 12582912 | tf_op jit(solution)/shard_map/dot_general | solution.py:8
  87.2 3.3 all-to-all-start
  90.5 4.1 all-to-all-done
  94.6 630.4 %all-gather.6.cloned.1.call-done = f32[8192,1024]{1,0:T(8,128)} async-done(((f32[1024,1024]{1,0:T(8,128)}), f32[8192,1024]{1,0:T(8,128)}) %all-gather.6.cloned.1.call-update) | async-done | bytes 33554448 | tf_op jit(solution)/shard_map/all_gather | solution.py:15
  725.0 14.7 %reduce_sum.9 = f32[1024,1024]{1,0:T(8,128)} reduce(f32[8,1024,1024]{2,1,0:T(8,128)} %bitcast.139, f32[]{:T(128)} %constant.276.clone.1), dimensions={0}, to_apply=%region_0.0 | reduce | flops 7340032 | bytes 37748740 | tf_op jit(solution)/shard_map/reduce_sum | solution.py:15
  739.7 5.6 copy.6
  745.3 4.4 fusion
  751.7 11.7 %cholesky.223 = f32[128,128]{1,0:T(8,128)S(1)} custom-call(f32[128,128]{1,0:T(8,128)S(1)} %cholesky.580), custom_call_target="Cholesky" | custom-call | tf_op jit(solution)/shard_map/jit(cholesky)/cholesky | solution.py:16
  763.4 2.5 cholesky.255
  765.9 9.8 custom-call.66
  775.7 2.4 constant_dynamic-update-slice_fusion.50
  779.7 12.2 %cholesky.244 = f32[128,128]{1,0:T(8,128)S(1)} custom-call(f32[128,128]{1,0:T(8,128)S(1)} %cholesky.584), custom_call_target="Cholesky" | custom-call | tf_op jit(solution)/shard_map/jit(cholesky)/cholesky | solution.py:16
  792.5 9.8 custom-call.67
  805.7 11.7 %cholesky.468 = f32[128,128]{1,0:T(8,128)S(1)} custom-call(f32[128,128]{1,0:T(8,128)S(1)} %cholesky.589), custom_call_target="Cholesky" | custom-call | tf_op jit(solution)/shard_map/jit(cholesky)/cholesky | solution.py:16
  818.7 9.8 custom-call.68
  829.7 2.3 convolution_subtract_fusion.2
  832.0 11.8 %cholesky.487 = f32[128,128]{1,0:T(8,128)S(1)} custom-call(f32[128,128]{1,0:T(8,128)S(1)} %cholesky.594), custom_call_target="Cholesky" | custom-call | tf_op jit(solution)/shard_map/jit(cholesky)/cholesky | solution.py:16
  845.2 9.8 custom-call.69
  856.1 2.3 convolution_subtract_fusion.3
  858.4 11.7 %cholesky.506 = f32[128,128]{1,0:T(8,128)S(1)} custom-call(f32[128,128]{1,0:T(8,128)S(1)} %cholesky.599), custom_call_target="Cholesky" | custom-call | tf_op jit(solution)/shard_map/jit(cholesky)/cholesky | solution.py:16
  871.4 10.0 custom-call.70
  882.4 2.3 convolution_subtract_fusion.4
  884.7 11.7 %cholesky.526 = f32[128,128]{1,0:T(8,128)S(1)} custom-call(f32[128,128]{1,0:T(8,128)S(1)} %cholesky.604), custom_call_target="Cholesky" | custom-call | tf_op jit(solution)/shard_map/jit(cholesky)/cholesky | solution.py:16
  897.7 9.8 custom-call.71
  910.5 12.1 %cholesky.546 = f32[128,128]{1,0:T(8,128)S(1)} custom-call(f32[128,128]{1,0:T(8,128)S(1)} %cholesky.609), custom_call_target="Cholesky" | custom-call | tf_op jit(solution)/shard_map/jit(cholesky)/cholesky | solution.py:16
  923.9 9.8 custom-call.72
  936.3 11.7 %cholesky.564 = f32[128,128]{1,0:T(8,128)S(1)} custom-call(f32[128,128]{1,0:T(8,128)S(1)} %convolution_subtract_fusion.6), custom_call_target="Cholesky" | custom-call | tf_op jit(solution)/shard_map/jit(cholesky)/cholesky | solution.py:16
  954.8 4.8 select_select_fusion
  959.6 22.8 %while.1 = (s32[]{:T(128)}, f32[1024,1024]{1,0:T(8,128)}, s32[8,2]{0,1:T(2,128)S(1)}, f32[8,128,128]{2,1,0:T(8,128)S(1)}, s32[]{:T(128)}) while((s32[]{:T(128)}, f32[1024,1024]{1,0:T(8,128)}, s32[8,2]{0,1:T(2,128)S(1)}, f32[8,128,128]{2,1,0:T(8,128)S(1)}, s32[]{:T(128)}) %tuple.56), condition=%wide.while_cond, body=%wide.while_body.sunk | while | flops 2 | bytes 131181 | solution.py:21
  982.5 78.8 %custom-call.73 = f32[8,128,128]{1,2,0:T(8,128)S(1)} custom-call(f32[8,128,128]{2,1,0:T(8,128)S(1)} %get-tuple-element.12), custom_call_target="InvertDiagBlocksLowerTriangular" | custom-call | tf_op jit(solution)/shard_map/jit(_cho_solve)/triangular_solve | solution.py:21
  (123 shorter events, 69.8 us)
Async XLA Ops:
  7.4 64.6 %all-gather.4.cloned.1.call-start = ((), (), s32[]{:S(2)}) async-start(), calls=%async_computation.2 | async-start | bytes 10485760 | tf_op jit(solution)/shard_map/all_gather | solution.py:14
  8.1 79.1 %reduce-scatter.2.cloned.1.call-start = ((), (), s32[]{:S(2)}) async-start(), calls=%async_computation.3 | async-start | bytes 589824 | tf_op jit(solution)/shard_map/reduce_scatter | solution.py:17
  13.1 711.9 %all-gather.6.cloned.1.call-start = ((), (), s32[]{:S(2)}) async-start(), calls=%async_computation.4 | async-start | bytes 37748736 | tf_op jit(solution)/shard_map/all_gather | solution.py:15
  87.2 7.4 all-to-all-start
  749.7 1.9 copy-start
  1082.2 0.6 copy-start.1
Sparse Core Ops, SparseCore 0:
  9.8 62.1 all-gather.3
Sparse Core Ops, SparseCore 1:
  13.2 64.7 reduce-scatter.1
  87.3 637.7 all-gather.5
